TPU v7x, 32 devices: a whole 2x2x4 slice. The times are simulated.
32 devices in a mesh: dp: 4 (over y, core), row: 2 (over x), col: 4 (over z).
Axes of the slice: x: 2, y: 2, z: 4, core: 2. Of those that a mesh axis runs over, the one named last changes fastest.
Arguments:
- layer_input: bfloat16 [12288, 1536], P(('dp', 'col'), 'row'), may hold values from -6 to 6
- attn_gain: float32 [1536], P('row'), may hold values from 0.25 to 1.75
- qkv_weight: bfloat16 [1536, 4608], P('row', 'col'), may hold values from -0.15625 to 0.15625
- forget_weight: bfloat16 [1536, 24], P('row', 'col'), may hold values from -0.15625 to 0.15625
- forget_bias: float32 [24], P('col'), may hold values from 2.5 to 7
- out_weight: bfloat16 [1536, 1536], P('col', 'row'), may hold values from -0.625 to 0.625
- ffn_gain: float32 [1536], P('row'), may hold values from 0.25 to 1.75
- gate_weight: bfloat16 [1536, 4096], P('row', 'col'), may hold values from -0.15625 to 0.15625
- up_weight: bfloat16 [1536, 4096], P('row', 'col'), may hold values from -0.15625 to 0.15625
- down_weight: bfloat16 [4096, 1536], P('col', 'row'), may hold values from -0.09375 to 0.09375
- prompt_doc: int32 [8, 1024], P(('dp', 'row')), may hold values from 0 to 3, never falling along the last dimension, each value on 1 to 512 neighbouring positions
- branch_seg: int32 [8, 512], P(('dp', 'row')), may hold values from 0 to 3, never falling along the last dimension, each value on 1 to 256 neighbouring positions
- branch_doc: int32 [8, 4], P(('dp', 'row')), may hold values from 0 to 3
- out_cotangent: bfloat16 [12288, 1536], P(('dp', 'col'), 'row'), may hold values from -6 to 6
Outputs:
- layer_output: bfloat16 [12288, 1536], P(('dp', 'col'), 'row')
- input_grad: bfloat16 [12288, 1536], P(('dp', 'col'), 'row')
- attn_gain_grad: float32 [1536], P('row')
- qkv_grad: float32 [1536, 4608], P('row', 'col')
- forget_grad: float32 [1536, 24], P('row', 'col')
- forget_bias_grad: float32 [24], P('col')
- out_grad: float32 [1536, 1536], P('col', 'row')
- ffn_gain_grad: float32 [1536], P('row')
- gate_grad: float32 [1536, 4096], P('row', 'col')
- up_grad: float32 [1536, 4096], P('row', 'col')
- down_grad: float32 [4096, 1536], P('col', 'row')
Inputs may be any that keep to these rules, and one draw needn't show every extreme that they name: `prompt_doc`: in each group the prompt's documents are numbered 0 to 3 in order, every one present, each of 1 to 512 tokens, one of exactly 512. `branch_seg`: in each group the continuations are numbered 0 to 3 in order, every one present, each of 1 to 256 tokens, one of exactly 256.
All inputs are finite; a program needn't handle non-finite values.
Results may differ from a plain program's by a relative error of at most 0.023.
Values may be sent and summed in bfloat16 or wider, within the bound.
A program may use at most 192 MiB of HBM per device.

v0:
```python
import jax
import jax.numpy as jnp
from jax import lax
from jax.sharding import PartitionSpec as P

D = 1536
DH = 64
DOCS = 4
QBLK = 512
EPS = 1e-06
MASKED = -1e30


def visible(row_start, doc_query, branch_query, doc_key, branch_key):
    pos_query = row_start + jnp.arange(doc_query.shape[0], dtype=jnp.int32)
    pos_key = jnp.arange(doc_key.shape[0], dtype=jnp.int32)
    causal = pos_key[None, :] <= pos_query[:, None]
    same_doc = doc_query[:, None] == doc_key[None, :]
    same_branch = (branch_key[None, :] < 0) | (branch_query[:, None] == branch_key[None, :])
    return causal & same_doc & same_branch


def decay_sums(log_rates, prompt_ids, branch_ids, branch_docs):
    prompt_len = prompt_ids.shape[0]
    prompt_part = log_rates[:prompt_len]
    branch_part = log_rates[prompt_len:]
    prompt_sums = jnp.cumsum(prompt_part, axis=0)
    doc_range = jnp.arange(DOCS, dtype=jnp.int32)
    doc_last = jnp.sum((prompt_ids[None, :] <= doc_range[:, None]).astype(jnp.int32), axis=1) - 1
    at_last = jnp.arange(prompt_len, dtype=jnp.int32)[None, :] == doc_last[:, None]
    doc_totals = jnp.sum(jnp.where(at_last[:, :, None], prompt_sums[None], 0.0), axis=1)
    branch_range = jnp.arange(branch_docs.shape[0], dtype=jnp.int32)
    picked = branch_docs[:, None] == doc_range[None, :]
    branch_start = jnp.sum(jnp.where(picked[:, :, None], doc_totals[None], 0.0), axis=1)
    earlier = branch_ids[None, :] < branch_range[:, None]
    skipped = jnp.sum(jnp.where(earlier[:, :, None], branch_part[None], 0.0), axis=1)
    member = branch_ids[:, None] == branch_range[None, :]
    offsets = jnp.sum(jnp.where(member[:, :, None], (branch_start - skipped)[None], 0.0), axis=1)
    decay_sum = jnp.concatenate([prompt_sums, jnp.cumsum(branch_part, axis=0) + offsets], axis=0)
    branch_doc_ids = jnp.sum(jnp.where(member, branch_docs[None, :], 0), axis=1)
    doc_ids = jnp.concatenate([prompt_ids, branch_doc_ids])
    branch_tags = jnp.concatenate([jnp.full((prompt_len,), -1, jnp.int32), branch_ids])
    return (decay_sum, doc_ids, branch_tags)


def block_scores(query_block, key_rows, decay_query, decay_key, allowed):
    raw_scores = jnp.einsum(
        "qhd,khd->hqk", query_block, key_rows, preferred_element_type=jnp.float32
    )
    scores = raw_scores * DH ** (-0.5) + decay_query.T[:, :, None] - decay_key.T[:, None, :]
    return jnp.where(allowed[None], scores, MASKED)


def contract_rows(left, right):
    return lax.dot_general(
        left, right, (((0,), (0,)), ((), ())), preferred_element_type=jnp.float32
    )


def contract_cols(left, right):
    return lax.dot_general(
        left, right, (((1,), (1,)), ((), ())), preferred_element_type=jnp.float32
    )


def row_stat(values):
    return lax.psum(values, "row")


def gather_tokens(token_rows):
    return lax.all_gather(token_rows, "col", axis=0, tiled=True)


def sum_tokens(partial_value):
    return lax.psum_scatter(
        partial_value.astype(jnp.bfloat16), "col", scatter_dimension=0, tiled=True
    ).astype(jnp.float32)


def gather_group(group_rows):
    return lax.all_gather(group_rows, "row", axis=0, tiled=True)


def sum_group(partial_value):
    return lax.psum_scatter(
        partial_value.astype(jnp.bfloat16), "row", scatter_dimension=0, tiled=True
    ).astype(jnp.float32)


def sum_pair(first, second):
    return (
        lax.psum_scatter(first, "row", scatter_dimension=0, tiled=True),
        lax.psum_scatter(second, "row", scatter_dimension=0, tiled=True),
    )


def gather_pair(first, second):
    return (
        lax.all_gather(first, "row", axis=0, tiled=True),
        lax.all_gather(second, "row", axis=0, tiled=True),
    )


def shards(
    layer_input,
    attn_gain,
    qkv_weight,
    forget_weight,
    forget_bias,
    out_weight,
    ffn_gain,
    gate_weight,
    up_weight,
    down_weight,
    prompt_doc,
    branch_seg,
    branch_doc,
    out_cotangent,
):
    score_scale = DH ** (-0.5)
    stream = layer_input.astype(jnp.float32)
    rms_a = lax.rsqrt(row_stat(jnp.sum(stream * stream, axis=1)) / D + EPS)[:, None]
    normed_a = (stream * rms_a * attn_gain).astype(jnp.bfloat16)
    normed_a_all = gather_tokens(normed_a)
    projected, forget_sum = sum_pair(
        jnp.dot(normed_a_all, qkv_weight, preferred_element_type=jnp.float32),
        jnp.dot(normed_a_all, forget_weight, preferred_element_type=jnp.float32),
    )
    group_len = projected.shape[0]
    heads = forget_weight.shape[1]
    qkv = projected.astype(jnp.bfloat16).reshape(group_len, heads, 3, DH)
    forget_logit = forget_sum + forget_bias
    log_rate = jax.nn.log_sigmoid(forget_logit)
    prompt_ids = prompt_doc[0]
    branch_ids = branch_seg[0]
    branch_docs = branch_doc[0]
    decay_sum, doc_ids, branch_tags = decay_sums(log_rate, prompt_ids, branch_ids, branch_docs)
    queries = qkv[:, :, 0]
    key_rows = qkv[:, :, 1]
    value_rows = qkv[:, :, 2]
    blocks = jnp.arange(group_len // QBLK, dtype=jnp.int32)

    def block_view(block_index):
        row_start = block_index * QBLK
        query_block = lax.dynamic_slice_in_dim(queries, row_start, QBLK, 0)
        decay_query = lax.dynamic_slice_in_dim(decay_sum, row_start, QBLK, 0)
        doc_query = lax.dynamic_slice_in_dim(doc_ids, row_start, QBLK, 0)
        branch_query = lax.dynamic_slice_in_dim(branch_tags, row_start, QBLK, 0)
        allowed = visible(row_start, doc_query, branch_query, doc_ids, branch_tags)
        scores = block_scores(query_block, key_rows, decay_query, decay_sum, allowed)
        return (row_start, query_block, scores)

    def forward_block(block_index):
        row_start, query_block, scores = block_view(block_index)
        row_max = jnp.max(scores, axis=2, keepdims=True)
        expo = jnp.exp(scores - row_max)
        row_total = jnp.sum(expo, axis=2, keepdims=True)
        probs = (expo / row_total).astype(jnp.bfloat16)
        attended_block = jnp.einsum(
            "hqk,khd->qhd", probs, value_rows, preferred_element_type=jnp.float32
        ).astype(jnp.bfloat16)
        return (attended_block, (row_max + jnp.log(row_total))[:, :, 0])

    attended_blocks, lse_blocks = lax.map(forward_block, blocks)
    attended = attended_blocks.reshape(group_len, heads * DH)
    attended_all = gather_group(attended)
    branch_out = sum_tokens(jnp.dot(attended_all, out_weight, preferred_element_type=jnp.float32))
    resid = stream + branch_out
    rms_b = lax.rsqrt(row_stat(jnp.sum(resid * resid, axis=1)) / D + EPS)[:, None]
    normed_b = (resid * rms_b * ffn_gain).astype(jnp.bfloat16)
    normed_b_all = gather_tokens(normed_b)
    gate_pre, up_pre = sum_pair(
        jnp.dot(normed_b_all, gate_weight, preferred_element_type=jnp.float32),
        jnp.dot(normed_b_all, up_weight, preferred_element_type=jnp.float32),
    )
    gate_sig = jax.nn.sigmoid(gate_pre)
    gate_act = gate_pre * gate_sig
    hidden = (gate_act * up_pre).astype(jnp.bfloat16)
    hidden_all = gather_group(hidden)
    layer_output = (
        resid + sum_tokens(jnp.dot(hidden_all, down_weight, preferred_element_type=jnp.float32))
    ).astype(jnp.bfloat16)
    cotangent = out_cotangent.astype(jnp.float32)
    cotangent_all = gather_tokens(out_cotangent)
    down_grad = contract_rows(hidden_all, cotangent_all)
    grad_hidden = sum_group(contract_cols(cotangent_all, down_weight))
    grad_gate = (grad_hidden * up_pre * gate_sig * (1.0 + gate_pre * (1.0 - gate_sig))).astype(
        jnp.bfloat16
    )
    grad_up = (grad_hidden * gate_act).astype(jnp.bfloat16)
    grad_gate_all, grad_up_all = gather_pair(grad_gate, grad_up)
    gate_grad = contract_rows(normed_b_all, grad_gate_all)
    up_grad = contract_rows(normed_b_all, grad_up_all)
    grad_normed_b = sum_tokens(
        contract_cols(grad_gate_all, gate_weight) + contract_cols(grad_up_all, up_weight)
    )
    gained_b = ffn_gain * grad_normed_b
    inner_b = row_stat(jnp.sum(resid * gained_b, axis=1))[:, None]
    ffn_gain_part = jnp.sum(grad_normed_b * resid * rms_b, axis=0)
    grad_resid = cotangent + rms_b * gained_b - resid * (rms_b * rms_b * rms_b) * inner_b / D
    grad_branch = grad_resid.astype(jnp.bfloat16)
    grad_branch_all = gather_tokens(grad_branch)
    out_grad = contract_rows(attended_all, grad_branch_all)
    attended_part = contract_cols(grad_branch_all, out_weight)
    grad_attended = sum_group(attended_part).astype(jnp.bfloat16).reshape(group_len, heads, DH)

    def back_block(carry, block_index):
        key_acc, value_acc, decay_keys = carry
        row_start, query_block, scores = block_view(block_index)
        grad_block = lax.dynamic_slice_in_dim(grad_attended, row_start, QBLK, 0)
        lse_block = lax.dynamic_index_in_dim(lse_blocks, block_index, 0, keepdims=False)
        probs_star = jnp.exp(scores - lse_block[:, :, None])
        grad_probs = jnp.einsum(
            "qhd,khd->hqk", grad_block, value_rows, preferred_element_type=jnp.float32
        )
        row_delta = jnp.sum(probs_star * grad_probs, axis=2, keepdims=True)
        grad_scores = (probs_star * (grad_probs - row_delta)).astype(jnp.bfloat16)
        grad_query = (
            jnp.einsum("hqk,khd->qhd", grad_scores, key_rows, preferred_element_type=jnp.float32)
            * score_scale
        )
        key_acc = key_acc + jnp.einsum(
            "hqk,qhd->khd", grad_scores, query_block, preferred_element_type=jnp.float32
        )
        value_acc = value_acc + jnp.einsum(
            "hqk,qhd->khd",
            probs_star.astype(jnp.bfloat16),
            grad_block,
            preferred_element_type=jnp.float32,
        )
        decay_rows = jnp.sum(grad_scores, axis=2, dtype=jnp.float32)
        decay_keys = decay_keys - jnp.sum(grad_scores, axis=1, dtype=jnp.float32)
        return ((key_acc, value_acc, decay_keys), (grad_query, decay_rows))

    zero_rows = jnp.zeros((group_len, heads, DH), jnp.float32)
    carried, stacked = lax.scan(
        back_block, (zero_rows, zero_rows, jnp.zeros((heads, group_len), jnp.float32)), blocks
    )
    key_acc, value_acc, decay_keys = carried
    query_blocks, decay_blocks = stacked
    grad_query = query_blocks.reshape(group_len, heads, DH)
    grad_decay = jnp.transpose(decay_blocks, (0, 2, 1)).reshape(group_len, heads) + decay_keys.T
    grad_qkv = (
        jnp.stack([grad_query, key_acc * score_scale, value_acc], axis=2)
        .astype(jnp.bfloat16)
        .reshape(group_len, heads * 3 * DH)
    )
    unused, pullback = jax.vjp(
        lambda log_rates: decay_sums(log_rates, prompt_ids, branch_ids, branch_docs)[0], log_rate
    )
    grad_log_rate = pullback(grad_decay)[0]
    grad_forget = (grad_log_rate * jax.nn.sigmoid(-forget_logit)).astype(jnp.bfloat16)
    grad_qkv_all, grad_forget_all = gather_pair(grad_qkv, grad_forget)
    qkv_grad = contract_rows(normed_a_all, grad_qkv_all)
    forget_grad = contract_rows(normed_a_all, grad_forget_all)
    forget_bias_grad = jnp.sum(grad_forget_all, axis=0, dtype=jnp.float32)
    grad_normed_a = sum_tokens(
        contract_cols(grad_qkv_all, qkv_weight) + contract_cols(grad_forget_all, forget_weight)
    )
    gained_a = attn_gain * grad_normed_a
    inner_a = row_stat(jnp.sum(stream * gained_a, axis=1))[:, None]
    attn_gain_part = jnp.sum(grad_normed_a * stream * rms_a, axis=0)
    input_grad = (
        grad_resid + rms_a * gained_a - stream * (rms_a * rms_a * rms_a) * inner_a / D
    ).astype(jnp.bfloat16)
    attn_gain_grad, ffn_gain_grad = lax.psum((attn_gain_part, ffn_gain_part), ("dp", "col"))
    summed = (
        lax.psum(qkv_grad.astype(jnp.bfloat16), "dp").astype(jnp.float32),
        lax.psum(forget_grad.astype(jnp.bfloat16), "dp").astype(jnp.float32),
        lax.psum(forget_bias_grad.astype(jnp.bfloat16), "dp").astype(jnp.float32),
        lax.psum(out_grad.astype(jnp.bfloat16), "dp").astype(jnp.float32),
        lax.psum(gate_grad.astype(jnp.bfloat16), "dp").astype(jnp.float32),
        lax.psum(up_grad.astype(jnp.bfloat16), "dp").astype(jnp.float32),
        lax.psum(down_grad.astype(jnp.bfloat16), "dp").astype(jnp.float32),
    )
    return (
        layer_output,
        input_grad,
        attn_gain_grad,
        summed[0],
        summed[1],
        summed[2],
        summed[3],
        ffn_gain_grad,
        summed[4],
        summed[5],
        summed[6],
    )


def solution(mesh):
    in_specs = (
        P(("dp", "col"), "row"),
        P("row"),
        P("row", "col"),
        P("row", "col"),
        P("col"),
        P("col", "row"),
        P("row"),
        P("row", "col"),
        P("row", "col"),
        P("col", "row"),
        P(("dp", "row"), None),
        P(("dp", "row"), None),
        P(("dp", "row"), None),
        P(("dp", "col"), "row"),
    )
    out_specs = (
        P(("dp", "col"), "row"),
        P(("dp", "col"), "row"),
        P("row"),
        P("row", "col"),
        P("row", "col"),
        P("col"),
        P("col", "row"),
        P("row"),
        P("row", "col"),
        P("row", "col"),
        P("col", "row"),
    )
    return jax.shard_map(shards, mesh=mesh, in_specs=in_specs, out_specs=out_specs, check_vma=False)
```

profile of v0, /device:TPU:0, one launch (start us, length us, event | category | flops | bytes accessed | tf_op | source)
XLA Modules:
  0.0 2115.4 jit_solution(11031045359977941894)
XLA Ops:
  8.9 5.8 psum.91
  18.7 91.3 %all-gather.10.cloned.1.call-done = bf16[3072,768]{1,0:T(8,128)(2,1)} async-done(((bf16[768,768]{1,0:T(8,128)(2,1)}), bf16[3072,768]{1,0:T(8,128)(2,1)}) %all-gather.10.cloned.1.call-update) | async-done | bytes 4718608 | tf_op jit(solution)/shard_map/all_gather | solution.py:71
  114.4 11.1 fusion.65
  132.6 154.2 %reduce-scatter.11.cloned.1.call-done = f32[1536,1152]{1,0:T(8,128)} async-done(((f32[3072,1152]{1,0:T(8,128)}), f32[1536,1152]{1,0:T(8,128)}) %reduce-scatter.11.cloned.1.call-update) | async-done | bytes 7077904 | tf_op jit(solution)/shard_map/reduce_scatter | solution.py:92
  286.8 5.2 convert_element_type.142
  292.0 5.7 copy.48
  301.6 77.2 %while.31 = (s32[]{:T(128)}, bf16[3,512,6,64]{1,3,2,0:T(8,128)(2,1)}, f32[3,6,512]{2,1,0:T(8,128)S(1)}, s32[3]{0:T(128)S(1)}, s32[1536]{0:T(1024)S(1)}, /*index=...) while((s32[]{:T(128)}, ...), condition=%wide.region_17.18_spmd, body=%wide.region_14.17_spmd.sunk | while | flops 1297808384 | bytes 66381052 | solution.py:164
  304.7 7.2 fusion.137
  311.9 6.5 fusion.138
  318.5 8.9 fusion.139
  330.3 7.2 fusion.137
  337.5 6.5 fusion.138
  344.1 8.9 fusion.139
  355.9 7.2 fusion.137
  363.1 6.5 fusion.138
  369.7 8.9 fusion.139
  382.5 36.2 %all-gather.12.cloned.1.call-done = bf16[3072,384]{0,1:T(8,128)(2,1)} async-done(((bf16[1536,384]{0,1:T(8,128)(2,1)}), bf16[3072,384]{0,1:T(8,128)(2,1)}) %all-gather.12.cloned.1.call-update) | async-done | bytes 2359312 | tf_op jit(solution)/shard_map/all_gather | solution.py:81
  418.7 6.4 convolution_convert_fusion.2
  425.8 84.8 %reduce-scatter.15.cloned.1.call-done = bf16[768,768]{1,0:T(8,128)(2,1)} async-done(((bf16[3072,768]{1,0:T(8,128)(2,1)}), bf16[768,768]{1,0:T(8,128)(2,1)}) %reduce-scatter.15.cloned.1.call-update) | async-done | bytes 1179664 | tf_op jit(solution)/shard_map/reduce_scatter | solution.py:75
  520.1 81.9 %all-gather.18.cloned.1.call-done = bf16[3072,768]{1,0:T(8,128)(2,1)} async-done(((bf16[768,768]{1,0:T(8,128)(2,1)}), bf16[3072,768]{1,0:T(8,128)(2,1)}) %all-gather.18.cloned.1.call-update) | async-done | bytes 4718608 | tf_op jit(solution)/shard_map/all_gather | solution.py:71
  602.0 9.7 convolution_convert_fusion
  611.7 80.3 %all-gather.14.cloned.1.call-done = bf16[3072,768]{1,0:T(8,128)(2,1)} async-done(((bf16[768,768]{1,0:T(8,128)(2,1)}), bf16[3072,768]{1,0:T(8,128)(2,1)}) %all-gather.14.cloned.1.call-update) | async-done | bytes 4718608 | tf_op jit(solution)/shard_map/all_gather | solution.py:71
  692.0 10.0 fusion.68
  702.1 10.4 fusion.67
  712.6 57.2 %reduce-scatter.23.cloned.1.call-done = bf16[1536,1024]{1,0:T(8,128)(2,1)} async-done(((bf16[3072,1024]{1,0:T(8,128)(2,1)}), bf16[1536,1024]{1,0:T(8,128)(2,1)}) %reduce-scatter.23.cloned.1.call-update) | async-done | bytes 3145744 | tf_op jit(solution)/shard_map/reduce_scatter | solution.py:85
  769.9 146.9 %reduce-scatter.19.cloned.1.call-done = f32[1536,1024]{1,0:T(8,128)} async-done(((f32[3072,1024]{1,0:T(8,128)}), f32[1536,1024]{1,0:T(8,128)}) %reduce-scatter.19.cloned.1.call-update) | async-done | bytes 6291472 | tf_op jit(solution)/shard_map/reduce_scatter | solution.py:93
  916.8 146.7 %reduce-scatter.17.cloned.1.call-done = f32[1536,1024]{1,0:T(8,128)} async-done(((f32[3072,1024]{1,0:T(8,128)}), f32[1536,1024]{1,0:T(8,128)}) %reduce-scatter.17.cloned.1.call-update) | async-done | bytes 6291472 | tf_op jit(solution)/shard_map/reduce_scatter | solution.py:92
  1063.5 9.9 fusion.37
  1074.1 79.9 %all-gather.20.cloned.1.call-done = bf16[3072,1024]{1,0:T(8,128)(2,1)} async-done(((bf16[1536,1024]{1,0:T(8,128)(2,1)}), bf16[3072,1024]{1,0:T(8,128)(2,1)}) %all-gather.20.cloned.1.call-update) | async-done | bytes 6291472 | tf_op jit(solution)/shard_map/all_gather | solution.py:99
  1154.0 10.0 fusion.69
  1164.1 72.4 %all-gather.22.cloned.1.call-done = bf16[3072,1024]{1,0:T(8,128)(2,1)} async-done(((bf16[1536,1024]{1,0:T(8,128)(2,1)}), bf16[3072,1024]{1,0:T(8,128)(2,1)}) %all-gather.22.cloned.1.call-update) | async-done | bytes 6291472 | tf_op jit(solution)/shard_map/all_gather | solution.py:100
  1236.5 10.6 add_convert_fusion.1
  1247.1 85.4 %reduce-scatter.25.cloned.1.call-done = bf16[768,768]{1,0:T(8,128)(2,1)} async-done(((bf16[3072,768]{1,0:T(8,128)(2,1)}), bf16[768,768]{1,0:T(8,128)(2,1)}) %reduce-scatter.25.cloned.1.call-update) | async-done | bytes 1179664 | tf_op jit(solution)/shard_map/reduce_scatter | solution.py:75
  1344.7 90.0 %all-gather.24.cloned.1.call-done = bf16[3072,768]{1,0:T(8,128)(2,1)} async-done(((bf16[768,768]{1,0:T(8,128)(2,1)}), bf16[3072,768]{1,0:T(8,128)(2,1)}) %all-gather.24.cloned.1.call-update) | async-done | bytes 4718608 | tf_op jit(solution)/shard_map/all_gather | solution.py:71
  1434.8 6.5 convolution_convert_fusion.3
  1442.1 32.5 %reduce-scatter.27.cloned.1.call-done = bf16[1536,384]{1,0:T(8,128)(2,1)} async-done(((bf16[3072,384]{1,0:T(8,128)(2,1)}), bf16[1536,384]{1,0:T(8,128)(2,1)}) %reduce-scatter.27.cloned.1.call-update) | async-done | bytes 1179664 | tf_op jit(solution)/shard_map/reduce_scatter | solution.py:85
  1477.0 203.3 %while.32 = (s32[]{:T(128)}, f32[1536,6,64]{0,2,1:T(8,128)}, f32[1536,6,64]{0,2,1:T(8,128)}, f32[6,1536]{1,0:T(8,128)S(1)}, bf16[3,512,6,64]{1,3,2,0:T(8,128)(2,...) while((s32[]{:T(128)}, f32[1536,6,64]{0,2,1:T(8,128)}, ...), condition=%wide.region_33.34_spmd.clone, body=%wide.region_29.33_spmd.clone.sunk | while | flops 3093238784 | bytes 276796800 | solution.py:236
  1481.9 10.7 fusion.149
  1492.7 15.2 multiply_reduce_fusion.3
  1507.9 16.3 convert_reduce_fusion.4
  1532.8 7.8 fusion.153
  1549.7 9.2 fusion.149
  1558.8 15.2 multiply_reduce_fusion.3
  1574.0 16.3 convert_reduce_fusion.4
  1594.6 5.2 fusion.152
  1599.8 7.8 fusion.153
  1617.5 9.2 fusion.149
  1626.6 15.2 multiply_reduce_fusion.3
  1641.8 16.3 convert_reduce_fusion.4
  1667.6 7.8 fusion.153
  1691.1 9.6 convolution_convert_fusion.6
  1700.7 10.4 convolution_convert_fusion.7
  1711.1 9.6 convolution_convert_fusion.5
  1726.5 7.4 reduce-window.36
  1734.3 46.6 %all-gather.26.cloned.1.call-done = bf16[3072,1152]{0,1:T(8,128)(2,1)} async-done(((bf16[1536,1152]{0,1:T(8,128)(2,1)}), bf16[3072,1152]{0,1:T(8,128)(2,1)}) %all-gather.26.cloned.1.call-update) | async-done | bytes 7077904 | tf_op jit(solution)/shard_map/all_gather | solution.py:99
  1780.9 11.2 convolution_convert_fusion.4
  1792.2 7.7 reduce-window.34
  1805.0 8.8 fusion.70
  1818.7 9.5 convolution_convert_fusion.1
  1831.5 12.0 all-reduce.4
  1844.6 81.0 %all-reduce.8.cloned.1.call-done = (bf16[768,1152]{1,0:T(8,128)(2,1)}, bf16[384,768]{1,0:T(8,128)(2,1)}, bf16[768,1024]{1,0:T(8,128)(2,1)}, bf16[768,1024]{1,0:T(8,128)(2,1)}, bf16[1024,768]{1,0:T(8,128)(2,1)}) async-done(((bf16[768,1152]{1,0:T(8,128)(2,1)}, bf16[384,768]{1,0:T(8,128)(2,1)}, bf16[768,1024]{1,0:T(8,128)(2,1)}, bf16[768,1024]{1,0:T(8,128)(2,1)}, bf16[1024,768]{1,0:T(8,128)(2,1)}), ...) | async-done | bytes 7077904 | tf_op jit(solution)/shard_map/psum | solution.py:268
  1935.9 77.4 %reduce-scatter.29.cloned.1.call-done = bf16[768,768]{1,0:T(8,128)(2,1)} async-done(((bf16[3072,768]{1,0:T(8,128)(2,1)}), bf16[768,768]{1,0:T(8,128)(2,1)}) %reduce-scatter.29.cloned.1.call-update) | async-done | bytes 1179664 | tf_op jit(solution)/shard_map/reduce_scatter | solution.py:75
  2015.7 36.5 %all-reduce.3 = (f32[768]{0:T(1024)}, f32[768]{0:T(1024)}) all-reduce(f32[768]{0:T(1024)S(1)} %get-tuple-element.219, f32[768]{0:T(1024)S(1)} %copy-done.35), channel_id=1, replica_groups=mesh['dp'=4,'row'=2,'col'=4] {'dp','col'}, use_global_device_ids=true, to_apply=%region_46.47 | all-reduce | flops 1536 | bytes 12288 | tf_op jit(solution)/shard_map/psum | solution.py:266
  2057.1 46.4 %reduce-scatter.21.cloned.1.call-done = bf16[768,768]{1,0:T(8,128)(2,1)} async-done(((bf16[3072,768]{1,0:T(8,128)(2,1)}), bf16[768,768]{1,0:T(8,128)(2,1)}) %reduce-scatter.21.cloned.1.call-update) | async-done | bytes 1179664 | tf_op jit(solution)/shard_map/reduce_scatter | solution.py:75
  (311 shorter events, 154.5 us)
Async XLA Ops:
  7.2 107.2 %copy-start = (bf16[768,1152]{1,0:T(8,128)(2,1)S(1)}, bf16[768,1152]{1,0:T(8,128)(2,1)}, u32[]{:S(2)}) copy-start(bf16[768,1152]{1,0:T(8,128)(2,1)} %param.20) | copy-start | bytes 5308420
  7.2 102.8 %copy-start.20 = (bf16[768,6]{0,1:T(8,128)(2,1)S(1)}, bf16[768,6]{0,1:T(8,128)(2,1)}, u32[]{:S(2)}) copy-start(bf16[768,6]{0,1:T(8,128)(2,1)} %param.21) | copy-start | bytes 27652
  7.2 102.8 %all-gather.10.cloned.1.call-start = ((), (), s32[]{:S(2)}) async-start(), calls=%async_computation.10 | async-start | bytes 5898240 | tf_op jit(solution)/shard_map/all_gather | solution.py:71
  18.6 108.0 %reduce-scatter.13.cloned.1.call-start = ((), (), s32[]{:S(2)}) async-start(), calls=%async_computation.12 | async-start | bytes 147456 | tf_op jit(solution)/shard_map/reduce_scatter | solution.py:93
  114.3 172.5 %reduce-scatter.11.cloned.1.call-start = ((), (), s32[]{:S(2)}) async-start(), calls=%async_computation.11 | async-start | bytes 21233664 | tf_op jit(solution)/shard_map/reduce_scatter | solution.py:92
  125.5 293.2 %all-gather.12.cloned.1.call-start = ((), (), s32[]{:S(2)}) async-start(), calls=%async_computation.13 | async-start | bytes 3538944 | tf_op jit(solution)/shard_map/all_gather | solution.py:81
  126.5 165.5 %copy-start.39 = (pred[4,4]{1,0:T(4,128)(4,1)}, pred[4,4]{1,0:T(4,128)(4,1)S(1)}, u32[]{:S(2)}) copy-start(pred[4,4]{1,0:T(4,128)(4,1)S(1)} %iota_compare_fusion.6) | copy-start | bytes 52
  126.5 3.7 copy-start.30
  126.5 6.0 copy-start.32
  126.6 3.6 copy-start.23
  304.6 7.3 copy-start.3
  330.2 7.3 copy-start.3
  355.8 7.3 copy-start.3
  381.1 37.6 %copy-start.44 = (bf16[384,768]{1,0:T(8,128)(2,1)S(1)}, bf16[384,768]{1,0:T(8,128)(2,1)}, u32[]{:S(2)}) copy-start(bf16[384,768]{1,0:T(8,128)(2,1)} %param.23) | copy-start | bytes 1769476
  382.5 128.1 %reduce-scatter.15.cloned.1.call-start = ((), (), s32[]{:S(2)}) async-start(), calls=%async_computation.14 | async-start | bytes 5898240 | tf_op jit(solution)/shard_map/reduce_scatter | solution.py:75
  425.2 85.5 %copy-start.4 = (bf16[768,768]{1,0:T(8,128)(2,1)S(1)}, bf16[768,768]{1,0:T(8,128)(2,1)}, u32[]{:S(2)}) copy-start(bf16[768,768]{1,0:T(8,128)(2,1)} %param.18) | copy-start | bytes 3538948
  425.2 92.1 %copy-start.18 = (f32[768]{0:T(1024)S(1)}, f32[768]{0:T(1024)}, u32[]{:S(2)}) copy-start(f32[768]{0:T(1024)} %param.24) | copy-start | bytes 9220
  425.2 176.8 %all-gather.18.cloned.1.call-start = ((), (), s32[]{:S(2)}) async-start(), calls=%async_computation.20 | async-start | bytes 5898240 | tf_op jit(solution)/shard_map/all_gather | solution.py:71
  425.8 266.3 %all-gather.14.cloned.1.call-start = ((), (), s32[]{:S(2)}) async-start(), calls=%async_computation.15 | async-start | bytes 5898240 | tf_op jit(solution)/shard_map/all_gather | solution.py:71
  517.3 823.4 %copy-start.14 = (f32[768]{0:T(1024)}, f32[768]{0:T(1024)S(1)}, u32[]{:S(2)}) copy-start(f32[768]{0:T(1024)S(1)} %get-tuple-element.300) | copy-start | bytes 9220
  517.3 823.4 %copy-start.25 = (f32[768]{0:T(1024)}, f32[768]{0:T(1024)S(1)}, u32[]{:S(2)}) copy-start(f32[768]{0:T(1024)S(1)} %get-tuple-element.299) | copy-start | bytes 9220
  520.1 249.8 %reduce-scatter.23.cloned.1.call-start = ((), (), s32[]{:S(2)}) async-start(), calls=%async_computation.21 | async-start | bytes 9437184 | tf_op jit(solution)/shard_map/reduce_scatter | solution.py:85
  611.7 305.1 %reduce-scatter.19.cloned.1.call-start = ((), (), s32[]{:S(2)}) async-start(), calls=%async_computation.17 | async-start | bytes 18874368 | tf_op jit(solution)/shard_map/reduce_scatter | solution.py:93
  702.1 361.5 %reduce-scatter.17.cloned.1.call-start = ((), (), s32[]{:S(2)}) async-start(), calls=%async_computation.16 | async-start | bytes 18874368 | tf_op jit(solution)/shard_map/reduce_scatter | solution.py:92
  712.6 441.4 %all-gather.20.cloned.1.call-start = ((), (), s32[]{:S(2)}) async-start(), calls=%async_computation.22 | async-start | bytes 9437184 | tf_op jit(solution)/shard_map/all_gather | solution.py:99
  1073.5 163.0 %all-gather.22.cloned.1.call-start = ((), (), s32[]{:S(2)}) async-start(), calls=%async_computation.23 | async-start | bytes 9437184 | tf_op jit(solution)/shard_map/all_gather | solution.py:100
  1074.1 258.4 %reduce-scatter.25.cloned.1.call-start = ((), (), s32[]{:S(2)}) async-start(), calls=%async_computation.24 | async-start | bytes 5898240 | tf_op jit(solution)/shard_map/reduce_scatter | solution.py:75
  1247.1 187.7 %all-gather.24.cloned.1.call-start = ((), (), s32[]{:S(2)}) async-start(), calls=%async_computation.25 | async-start | bytes 5898240 | tf_op jit(solution)/shard_map/all_gather | solution.py:71
  1340.7 4.0 copy-start.27
  1344.7 130.0 %reduce-scatter.27.cloned.1.call-start = ((), (), s32[]{:S(2)}) async-start(), calls=%async_computation.26 | async-start | bytes 3538944 | tf_op jit(solution)/shard_map/reduce_scatter | solution.py:85
  1441.3 269.8 %all-gather.16.cloned.1.call-start = ((), (), s32[]{:S(2)}) async-start(), calls=%async_computation.18 | async-start | bytes 9437184 | tf_op jit(solution)/shard_map/all_gather | solution.py:81
  1441.4 35.6 %copy-start.6 = (bf16[1536,6,64]{0,2,1:T(8,128)(2,1)S(1)}, bf16[1536,6,64]{0,2,1:T(8,128)(2,1)}, u32[]{:S(2)}) copy-start(bf16[1536,6,64]{0,2,1:T(8,128)(2,1)} %get-tuple-element.600) | copy-start | bytes 3538948
  1441.9 338.9 %all-gather.26.cloned.1.call-start = ((), (), s32[]{:S(2)}) async-start(), calls=%async_computation.27 | async-start | bytes 10616832 | tf_op jit(solution)/shard_map/all_gather | solution.py:99
  1481.9 10.8 copy-start.12
  1507.9 20.6 copy-start.1
  1532.8 7.8 copy-start.2
  1549.7 9.2 copy-start.12
  1574.0 20.6 copy-start.1
  1599.8 7.8 copy-start.2
  1617.5 9.2 copy-start.12
  1641.8 20.6 copy-start.1
  1667.6 7.8 copy-start.2
  1685.7 2.9 copy-start.7
  1691.1 234.5 %all-reduce.8.cloned.1.call-start = ((), (), s32[]{:S(2)}) async-start(), calls=%async_computation.29 | async-start | bytes 14155776 | tf_op jit(solution)/shard_map/psum | solution.py:268
  1711.1 9.7 copy-start.42
  1720.7 5.2 copy-start.33
  1720.7 5.4 copy-start.40
  1720.8 5.6 copy-start.24
  1792.0 8.2 copy-start.31
  1792.0 8.4 copy-start.13
  1792.0 8.4 copy-start.38
  1792.0 221.3 %reduce-scatter.29.cloned.1.call-start = ((), (), s32[]{:S(2)}) async-start(), calls=%async_computation.28 | async-start | bytes 5898240 | tf_op jit(solution)/shard_map/reduce_scatter | solution.py:75
  1805.0 8.8 copy-start.21
  1817.4 286.2 %reduce-scatter.21.cloned.1.call-start = ((), (), s32[]{:S(2)}) async-start(), calls=%async_computation.19 | async-start | bytes 5898240 | tf_op jit(solution)/shard_map/reduce_scatter | solution.py:75
  1925.6 2.3 copy-start.8
  1934.0 79.3 %copy-start.5 = (bf16[768,768]{1,0:T(8,128)(2,1)S(1)}, bf16[768,768]{1,0:T(8,128)(2,1)}, u32[]{:S(2)}) copy-start(bf16[768,768]{1,0:T(8,128)(2,1)} %param.18) | copy-start | bytes 3538948
  1934.0 79.3 %copy-start.17 = (f32[768]{0:T(1024)S(1)}, f32[768]{0:T(1024)}, u32[]{:S(2)}) copy-start(f32[768]{0:T(1024)} %copy-done.16) | copy-start | bytes 9220
  1934.0 79.3 %copy-start.22 = (f32[768]{0:T(1024)S(1)}, f32[768]{0:T(1024)}, u32[]{:S(2)}) copy-start(f32[768]{0:T(1024)} %param.19) | copy-start | bytes 9220
  1935.9 79.8 %copy-start.35 = (f32[768]{0:T(1024)S(1)}, f32[768]{0:T(1024)}, u32[]{:S(2)}) copy-start(f32[768]{0:T(1024)} %get-tuple-element.217) | copy-start | bytes 9220
  1935.9 167.6 %copy-start.15 = (f32[768]{0:T(1024)S(1)}, f32[768]{0:T(1024)}, u32[]{:S(2)}) copy-start(f32[768]{0:T(1024)} %copy-done.14) | copy-start | bytes 9220
  1935.9 167.6 %copy-start.19 = (f32[768]{0:T(1024)S(1)}, f32[768]{0:T(1024)}, u32[]{:S(2)}) copy-start(f32[768]{0:T(1024)} %param.24) | copy-start | bytes 9220
  1935.9 167.6 %copy-start.26 = (f32[768]{0:T(1024)S(1)}, f32[768]{0:T(1024)}, u32[]{:S(2)}) copy-start(f32[768]{0:T(1024)} %copy-done.25) | copy-start | bytes 9220
  1935.9 167.6 %copy-start.28 = (f32[768]{0:T(1024)S(1)}, f32[768]{0:T(1024)}, u32[]{:S(2)}) copy-start(f32[768]{0:T(1024)} %copy-done.27) | copy-start | bytes 9220
  1935.9 167.6 %copy-start.34 = (f32[768]{0:T(1024)S(1)}, f32[768]{0:T(1024)}, u32[]{:S(2)}) copy-start(f32[768]{0:T(1024)} %get-tuple-element.297) | copy-start | bytes 9220
  (9 other events, 11.4 us)
Sparse Core Ops, SparseCore 0:
  18.7 91.2 all-gather.9
  114.4 8.4 reduce-scatter.12
  125.6 161.1 reduce-scatter.10
  382.6 36.0 all-gather.11
  425.3 85.2 reduce-scatter.14
  512.0 89.9 all-gather.17
  604.1 87.8 all-gather.13
  694.3 75.5 reduce-scatter.22
  772.3 144.4 reduce-scatter.18
  919.1 144.4 reduce-scatter.16
  1073.6 80.3 all-gather.19
  1156.1 80.3 all-gather.21
  1247.2 85.2 reduce-scatter.24
  1344.8 89.9 all-gather.23
  1441.5 33.1 reduce-scatter.26
  1476.6 80.3 all-gather.15
  1691.2 89.5 all-gather.25
  1792.2 133.3 all-reduce.7
  1927.9 85.4 reduce-scatter.28
  2015.5 87.9 reduce-scatter.20
where the time goes:
time: 2120 us
  waiting for transfers between devices  1490 us (70%)
  matrix products  325 us (15%)
  other arithmetic  153 us (7%)
  blocking collectives  73.6 us (3%)
  local copies, waits for them, and re-layouts  44.4 us (2%)
    all_gather x4, waiting for transfers between devices, gather_tokens(): return lax.all_gather(token_rows, 'col', axis=0, tiled=True)  344 us
    reduce_scatter x2, waiting for transfers between devices, sum_pair(): lax.psum_scatter(first, 'row', scatter_dimension=0, tiled=True)  301 us
    reduce_scatter x4, waiting for transfers between devices, sum_tokens(): lax.psum_scatter(partial_value.astype(jnp.bfloat16), 'col', scatter_dimen...  294 us
    reduce_scatter x2, waiting for transfers between devices, sum_pair(): lax.psum_scatter(second, 'row', scatter_dimension=0, tiled=True)  147 us
    all_gather x2, waiting for transfers between devices, gather_pair(): lax.all_gather(first, 'row', axis=0, tiled=True)  127 us
    reduce_scatter x2, waiting for transfers between devices, sum_group(): lax.psum_scatter(partial_value.astype(jnp.bfloat16), 'row', scatter_dimen...  89.7 us
    psum x1, waiting for transfers between devices, shards(): lax.psum(qkv_grad.astype(jnp.bfloat16), 'dp').astype(jnp.float32)  81 us
    all_gather x1, waiting for transfers between devices, gather_pair(): lax.all_gather(second, 'row', axis=0, tiled=True)  72.4 us
  transfers between devices with their start and end apart: 20, of which 18 were waited for; matrix products, arithmetic and copies ran while one was open for 16% of the time, Pallas kernels for 0%

commit v1 on v0

--- a/solution.py
+++ b/solution.py
@@ -265,7 +265,7 @@
     ).astype(jnp.bfloat16)
     attn_gain_grad, ffn_gain_grad = lax.psum((attn_gain_part, ffn_gain_part), ("dp", "col"))
     summed = (
-        lax.psum(qkv_grad.astype(jnp.bfloat16), "dp").astype(jnp.float32),
+        jnp.sum(lax.all_gather(qkv_grad.astype(jnp.bfloat16), "dp"), axis=0).astype(jnp.float32),
         lax.psum(forget_grad.astype(jnp.bfloat16), "dp").astype(jnp.float32),
         lax.psum(forget_bias_grad.astype(jnp.bfloat16), "dp").astype(jnp.float32),
         lax.psum(out_grad.astype(jnp.bfloat16), "dp").astype(jnp.float32),

time: 2120 us -> 2140 us (level)
    all_gather x0 -> x1, waiting for transfers between devices: none -> 48.9 us  [shards(): lax.all_gather(qkv_grad.astype(jnp.bfloat16), 'dp')]
  transfers between devices with their start and end apart: 20 -> 21, of which waited for: 18 -> 19; matrix products, arithmetic and copies ran while one was open for 16% -> 17% of each run, Pallas kernels for 0% -> 0%
where the time goes in v1:
time: 2140 us; the launch traced here: 2130 us
  waiting for transfers between devices  1510 us (71%)
  matrix products  325 us (15%)
  other arithmetic  158 us (7%)
  blocking collectives  73.8 us (3%)
  local copies, waits for them, and re-layouts  43.5 us (2%)
    all_gather x4, waiting for transfers between devices, gather_tokens(): return lax.all_gather(token_rows, 'col', axis=0, tiled=True)  344 us
    reduce_scatter x2, waiting for transfers between devices, sum_pair(): lax.psum_scatter(first, 'row', scatter_dimension=0, tiled=True)  301 us
    reduce_scatter x4, waiting for transfers between devices, sum_tokens(): lax.psum_scatter(partial_value.astype(jnp.bfloat16), 'col', scatter_dimen...  280 us
    reduce_scatter x2, waiting for transfers between devices, sum_pair(): lax.psum_scatter(second, 'row', scatter_dimension=0, tiled=True)  147 us
    all_gather x2, waiting for transfers between devices, gather_pair(): lax.all_gather(first, 'row', axis=0, tiled=True)  113 us
    reduce_scatter x2, waiting for transfers between devices, sum_group(): lax.psum_scatter(partial_value.astype(jnp.bfloat16), 'row', scatter_dimen...  89.7 us
    psum x1, waiting for transfers between devices, shards(): lax.psum(out_grad.astype(jnp.bfloat16), 'dp').astype(jnp.float32)  74.8 us
    all_gather x1, waiting for transfers between devices, gather_pair(): lax.all_gather(second, 'row', axis=0, tiled=True)  72.4 us
  transfers between devices with their start and end apart: 21, of which 19 were waited for; matrix products, arithmetic and copies ran while one was open for 17% of the time, Pallas kernels for 0%

profile of v1, /device:TPU:0, one launch (start us, length us, event | category | flops | bytes accessed | tf_op | source)
XLA Modules:
  0.0 2135.0 jit_solution(3044214438286862150)
XLA Ops:
  8.9 5.8 psum.84
  18.7 91.3 %all-gather.12.cloned.1.call-done = bf16[3072,768]{1,0:T(8,128)(2,1)} async-done(((bf16[768,768]{1,0:T(8,128)(2,1)}), bf16[3072,768]{1,0:T(8,128)(2,1)}) %all-gather.12.cloned.1.call-update) | async-done | bytes 4718608 | tf_op jit(solution)/shard_map/all_gather | solution.py:71
  114.4 11.1 fusion.65
  132.6 154.2 %reduce-scatter.11.cloned.1.call-done = f32[1536,1152]{1,0:T(8,128)} async-done(((f32[3072,1152]{1,0:T(8,128)}), f32[1536,1152]{1,0:T(8,128)}) %reduce-scatter.11.cloned.1.call-update) | async-done | bytes 7077904 | tf_op jit(solution)/shard_map/reduce_scatter | solution.py:92
  292.0 5.7 copy.48
  301.6 77.2 %while.31 = (s32[]{:T(128)}, bf16[3,512,6,64]{1,3,2,0:T(8,128)(2,1)}, f32[3,6,512]{2,1,0:T(8,128)S(1)}, s32[3]{0:T(128)S(1)}, s32[1536]{0:T(1024)S(1)}, /*index=...) while((s32[]{:T(128)}, ...), condition=%wide.region_17.18_spmd, body=%wide.region_14.17_spmd.sunk | while | flops 1297808384 | bytes 66381052 | solution.py:164
  304.7 7.2 fusion.137
  311.9 6.5 fusion.138
  318.5 8.9 fusion.139
  330.3 7.2 fusion.137
  337.5 6.5 fusion.138
  344.1 8.9 fusion.139
  355.9 7.2 fusion.137
  363.1 6.5 fusion.138
  369.7 8.9 fusion.139
  382.5 36.2 %all-gather.14.cloned.1.call-done = bf16[3072,384]{0,1:T(8,128)(2,1)} async-done(((bf16[1536,384]{0,1:T(8,128)(2,1)}), bf16[3072,384]{0,1:T(8,128)(2,1)}) %all-gather.14.cloned.1.call-update) | async-done | bytes 2359312 | tf_op jit(solution)/shard_map/all_gather | solution.py:81
  418.7 6.4 convolution_convert_fusion.2
  425.8 84.8 %reduce-scatter.15.cloned.1.call-done = bf16[768,768]{1,0:T(8,128)(2,1)} async-done(((bf16[3072,768]{1,0:T(8,128)(2,1)}), bf16[768,768]{1,0:T(8,128)(2,1)}) %reduce-scatter.15.cloned.1.call-update) | async-done | bytes 1179664 | tf_op jit(solution)/shard_map/reduce_scatter | solution.py:75
  520.1 81.9 %all-gather.20.cloned.1.call-done = bf16[3072,768]{1,0:T(8,128)(2,1)} async-done(((bf16[768,768]{1,0:T(8,128)(2,1)}), bf16[3072,768]{1,0:T(8,128)(2,1)}) %all-gather.20.cloned.1.call-update) | async-done | bytes 4718608 | tf_op jit(solution)/shard_map/all_gather | solution.py:71
  602.0 9.7 convolution_convert_fusion
  611.7 80.3 %all-gather.16.cloned.1.call-done = bf16[3072,768]{1,0:T(8,128)(2,1)} async-done(((bf16[768,768]{1,0:T(8,128)(2,1)}), bf16[3072,768]{1,0:T(8,128)(2,1)}) %all-gather.16.cloned.1.call-update) | async-done | bytes 4718608 | tf_op jit(solution)/shard_map/all_gather | solution.py:71
  692.0 10.0 fusion.68
  702.1 10.4 fusion.67
  712.6 57.2 %reduce-scatter.23.cloned.1.call-done = bf16[1536,1024]{1,0:T(8,128)(2,1)} async-done(((bf16[3072,1024]{1,0:T(8,128)(2,1)}), bf16[1536,1024]{1,0:T(8,128)(2,1)}) %reduce-scatter.23.cloned.1.call-update) | async-done | bytes 3145744 | tf_op jit(solution)/shard_map/reduce_scatter | solution.py:85
  769.9 146.9 %reduce-scatter.19.cloned.1.call-done = f32[1536,1024]{1,0:T(8,128)} async-done(((f32[3072,1024]{1,0:T(8,128)}), f32[1536,1024]{1,0:T(8,128)}) %reduce-scatter.19.cloned.1.call-update) | async-done | bytes 6291472 | tf_op jit(solution)/shard_map/reduce_scatter | solution.py:93
  916.8 146.7 %reduce-scatter.17.cloned.1.call-done = f32[1536,1024]{1,0:T(8,128)} async-done(((f32[3072,1024]{1,0:T(8,128)}), f32[1536,1024]{1,0:T(8,128)}) %reduce-scatter.17.cloned.1.call-update) | async-done | bytes 6291472 | tf_op jit(solution)/shard_map/reduce_scatter | solution.py:92
  1063.5 9.9 fusion.37
  1074.1 79.9 %all-gather.22.cloned.1.call-done = bf16[3072,1024]{1,0:T(8,128)(2,1)} async-done(((bf16[1536,1024]{1,0:T(8,128)(2,1)}), bf16[3072,1024]{1,0:T(8,128)(2,1)}) %all-gather.22.cloned.1.call-update) | async-done | bytes 6291472 | tf_op jit(solution)/shard_map/all_gather | solution.py:99
  1154.0 10.0 fusion.69
  1164.1 72.4 %all-gather.24.cloned.1.call-done = bf16[3072,1024]{1,0:T(8,128)(2,1)} async-done(((bf16[1536,1024]{1,0:T(8,128)(2,1)}), bf16[3072,1024]{1,0:T(8,128)(2,1)}) %all-gather.24.cloned.1.call-update) | async-done | bytes 6291472 | tf_op jit(solution)/shard_map/all_gather | solution.py:100
  1236.5 10.6 add_convert_fusion.1
  1247.1 85.4 %reduce-scatter.25.cloned.1.call-done = bf16[768,768]{1,0:T(8,128)(2,1)} async-done(((bf16[3072,768]{1,0:T(8,128)(2,1)}), bf16[768,768]{1,0:T(8,128)(2,1)}) %reduce-scatter.25.cloned.1.call-update) | async-done | bytes 1179664 | tf_op jit(solution)/shard_map/reduce_scatter | solution.py:75
  1344.7 90.0 %all-gather.26.cloned.1.call-done = bf16[3072,768]{1,0:T(8,128)(2,1)} async-done(((bf16[768,768]{1,0:T(8,128)(2,1)}), bf16[3072,768]{1,0:T(8,128)(2,1)}) %all-gather.26.cloned.1.call-update) | async-done | bytes 4718608 | tf_op jit(solution)/shard_map/all_gather | solution.py:71
  1434.8 6.5 convolution_convert_fusion.3
  1442.1 32.5 %reduce-scatter.27.cloned.1.call-done = bf16[1536,384]{1,0:T(8,128)(2,1)} async-done(((bf16[3072,384]{1,0:T(8,128)(2,1)}), bf16[1536,384]{1,0:T(8,128)(2,1)}) %reduce-scatter.27.cloned.1.call-update) | async-done | bytes 1179664 | tf_op jit(solution)/shard_map/reduce_scatter | solution.py:85
  1477.0 203.3 %while.32 = (s32[]{:T(128)}, f32[1536,6,64]{0,2,1:T(8,128)}, f32[1536,6,64]{0,2,1:T(8,128)}, f32[6,1536]{1,0:T(8,128)S(1)}, bf16[3,512,6,64]{1,3,2,0:T(8,128)(2,...) while((s32[]{:T(128)}, f32[1536,6,64]{0,2,1:T(8,128)}, ...), condition=%wide.region_33.34_spmd.clone, body=%wide.region_29.33_spmd.clone.sunk | while | flops 3093238784 | bytes 276796800 | solution.py:236
  1481.9 10.7 fusion.149
  1492.7 15.2 multiply_reduce_fusion.3
  1507.9 16.3 convert_reduce_fusion.4
  1532.8 7.8 fusion.153
  1549.7 9.2 fusion.149
  1558.8 15.2 multiply_reduce_fusion.3
  1574.0 16.3 convert_reduce_fusion.4
  1599.8 7.8 fusion.153
  1617.5 9.2 fusion.149
  1626.6 15.2 multiply_reduce_fusion.3
  1641.8 16.3 convert_reduce_fusion.4
  1667.6 7.8 fusion.153
  1691.0 9.5 convolution_convert_fusion.6
  1700.4 10.4 convolution_convert_fusion.7
  1710.8 9.6 convolution_convert_fusion.5
  1726.7 7.5 reduce-window.34
  1734.9 7.4 reduce-window.36
  1747.9 33.3 %all-gather.28.cloned.1.call-done = bf16[3072,1152]{0,1:T(8,128)(2,1)} async-done(((bf16[1536,1152]{0,1:T(8,128)(2,1)}), bf16[3072,1152]{0,1:T(8,128)(2,1)}) %all-gather.28.cloned.1.call-update) | async-done | bytes 7077904 | tf_op jit(solution)/shard_map/all_gather | solution.py:99
  1781.2 9.0 fusion.70
  1793.9 9.0 convolution_convert_fusion.1
  1802.9 11.3 convolution_convert_fusion.4
  1814.2 74.8 %all-reduce.8.cloned.1.call-done = (bf16[384,768]{1,0:T(8,128)(2,1)}, bf16[768,1024]{1,0:T(8,128)(2,1)}, bf16[768,1024]{1,0:T(8,128)(2,1)}, bf16[1024,768]{1,0:T(8,128)(2,1)}) async-done(((bf16[384,768]{1,0:T(8,128)(2,1)}, bf16[768,1024]{1,0:T(8,128)(2,1)}, bf16[768,1024]{1,0:T(8,128)(2,1)}, bf16[1024,768]{1,0:T(8,128)(2,1)}), (bf16[384,768]{1,0:T(8,128)(2,1)}, bf16[768,1024]{1,0:T(8,128)(2,1)}, ...) | async-done | bytes 5308432 | tf_op jit(solution)/shard_map/psum | solution.py:271
  1901.0 11.7 all-reduce.4
  1913.8 63.1 %reduce-scatter.29.cloned.1.call-done = bf16[768,768]{1,0:T(8,128)(2,1)} async-done(((bf16[3072,768]{1,0:T(8,128)(2,1)}), bf16[768,768]{1,0:T(8,128)(2,1)}) %reduce-scatter.29.cloned.1.call-update) | async-done | bytes 1179664 | tf_op jit(solution)/shard_map/reduce_scatter | solution.py:75
  1979.2 36.5 %all-reduce.3 = (f32[768]{0:T(1024)}, f32[768]{0:T(1024)}) all-reduce(f32[768]{0:T(1024)S(1)} %get-tuple-element.219, f32[768]{0:T(1024)S(1)} %copy-done.34), channel_id=1, replica_groups=mesh['dp'=4,'row'=2,'col'=4] {'dp','col'}, use_global_device_ids=true, to_apply=%region_46.47 | all-reduce | flops 1536 | bytes 12288 | tf_op jit(solution)/shard_map/psum | solution.py:266
  2020.7 46.4 %reduce-scatter.21.cloned.1.call-done = bf16[768,768]{1,0:T(8,128)(2,1)} async-done(((bf16[3072,768]{1,0:T(8,128)(2,1)}), bf16[768,768]{1,0:T(8,128)(2,1)}) %reduce-scatter.21.cloned.1.call-update) | async-done | bytes 1179664 | tf_op jit(solution)/shard_map/reduce_scatter | solution.py:75
  2071.9 48.9 %all-gather.30.cloned.1.call-done = bf16[3072,1152]{1,0:T(8,128)(2,1)} async-done(((bf16[768,1152]{1,0:T(8,128)(2,1)}), bf16[3072,1152]{1,0:T(8,128)(2,1)}) %all-gather.30.cloned.1.call-update) | async-done | bytes 7077904 | tf_op jit(solution)/shard_map/all_gather | solution.py:268
  2120.7 5.2 reduce_sum.243
  (311 shorter events, 164.8 us)
Async XLA Ops:
  7.2 107.2 %copy-start = (bf16[768,1152]{1,0:T(8,128)(2,1)S(1)}, bf16[768,1152]{1,0:T(8,128)(2,1)}, u32[]{:S(2)}) copy-start(bf16[768,1152]{1,0:T(8,128)(2,1)} %param.20) | copy-start | bytes 5308420
  7.2 102.8 %copy-start.19 = (bf16[768,6]{0,1:T(8,128)(2,1)S(1)}, bf16[768,6]{0,1:T(8,128)(2,1)}, u32[]{:S(2)}) copy-start(bf16[768,6]{0,1:T(8,128)(2,1)} %param.21) | copy-start | bytes 27652
  7.2 102.8 %all-gather.12.cloned.1.call-start = ((), (), s32[]{:S(2)}) async-start(), calls=%async_computation.10 | async-start | bytes 5898240 | tf_op jit(solution)/shard_map/all_gather | solution.py:71
  18.6 108.0 %reduce-scatter.13.cloned.1.call-start = ((), (), s32[]{:S(2)}) async-start(), calls=%async_computation.12 | async-start | bytes 147456 | tf_op jit(solution)/shard_map/reduce_scatter | solution.py:93
  114.3 172.5 %reduce-scatter.11.cloned.1.call-start = ((), (), s32[]{:S(2)}) async-start(), calls=%async_computation.11 | async-start | bytes 21233664 | tf_op jit(solution)/shard_map/reduce_scatter | solution.py:92
  125.5 293.2 %all-gather.14.cloned.1.call-start = ((), (), s32[]{:S(2)}) async-start(), calls=%async_computation.13 | async-start | bytes 3538944 | tf_op jit(solution)/shard_map/all_gather | solution.py:81
  126.5 165.5 %copy-start.38 = (pred[4,4]{1,0:T(4,128)(4,1)}, pred[4,4]{1,0:T(4,128)(4,1)S(1)}, u32[]{:S(2)}) copy-start(pred[4,4]{1,0:T(4,128)(4,1)S(1)} %iota_compare_fusion.6) | copy-start | bytes 52
  126.5 3.7 copy-start.29
  126.5 6.0 copy-start.31
  126.6 3.6 copy-start.22
  304.6 7.3 copy-start.3
  330.2 7.3 copy-start.3
  355.8 7.3 copy-start.3
  381.1 37.6 %copy-start.42 = (bf16[384,768]{1,0:T(8,128)(2,1)S(1)}, bf16[384,768]{1,0:T(8,128)(2,1)}, u32[]{:S(2)}) copy-start(bf16[384,768]{1,0:T(8,128)(2,1)} %param.23) | copy-start | bytes 1769476
  382.5 128.1 %reduce-scatter.15.cloned.1.call-start = ((), (), s32[]{:S(2)}) async-start(), calls=%async_computation.14 | async-start | bytes 5898240 | tf_op jit(solution)/shard_map/reduce_scatter | solution.py:75
  425.2 85.5 %copy-start.4 = (bf16[768,768]{1,0:T(8,128)(2,1)S(1)}, bf16[768,768]{1,0:T(8,128)(2,1)}, u32[]{:S(2)}) copy-start(bf16[768,768]{1,0:T(8,128)(2,1)} %param.18) | copy-start | bytes 3538948
  425.2 92.1 %copy-start.17 = (f32[768]{0:T(1024)S(1)}, f32[768]{0:T(1024)}, u32[]{:S(2)}) copy-start(f32[768]{0:T(1024)} %param.24) | copy-start | bytes 9220
  425.2 176.8 %all-gather.20.cloned.1.call-start = ((), (), s32[]{:S(2)}) async-start(), calls=%async_computation.20 | async-start | bytes 5898240 | tf_op jit(solution)/shard_map/all_gather | solution.py:71
  425.8 266.3 %all-gather.16.cloned.1.call-start = ((), (), s32[]{:S(2)}) async-start(), calls=%async_computation.15 | async-start | bytes 5898240 | tf_op jit(solution)/shard_map/all_gather | solution.py:71
  517.3 823.4 %copy-start.13 = (f32[768]{0:T(1024)}, f32[768]{0:T(1024)S(1)}, u32[]{:S(2)}) copy-start(f32[768]{0:T(1024)S(1)} %get-tuple-element.299) | copy-start | bytes 9220
  517.3 823.4 %copy-start.24 = (f32[768]{0:T(1024)}, f32[768]{0:T(1024)S(1)}, u32[]{:S(2)}) copy-start(f32[768]{0:T(1024)S(1)} %get-tuple-element.298) | copy-start | bytes 9220
  520.1 249.8 %reduce-scatter.23.cloned.1.call-start = ((), (), s32[]{:S(2)}) async-start(), calls=%async_computation.21 | async-start | bytes 9437184 | tf_op jit(solution)/shard_map/reduce_scatter | solution.py:85
  611.7 305.1 %reduce-scatter.19.cloned.1.call-start = ((), (), s32[]{:S(2)}) async-start(), calls=%async_computation.17 | async-start | bytes 18874368 | tf_op jit(solution)/shard_map/reduce_scatter | solution.py:93
  702.1 361.5 %reduce-scatter.17.cloned.1.call-start = ((), (), s32[]{:S(2)}) async-start(), calls=%async_computation.16 | async-start | bytes 18874368 | tf_op jit(solution)/shard_map/reduce_scatter | solution.py:92
  712.6 441.4 %all-gather.22.cloned.1.call-start = ((), (), s32[]{:S(2)}) async-start(), calls=%async_computation.22 | async-start | bytes 9437184 | tf_op jit(solution)/shard_map/all_gather | solution.py:99
  1073.5 163.0 %all-gather.24.cloned.1.call-start = ((), (), s32[]{:S(2)}) async-start(), calls=%async_computation.23 | async-start | bytes 9437184 | tf_op jit(solution)/shard_map/all_gather | solution.py:100
  1074.1 258.4 %reduce-scatter.25.cloned.1.call-start = ((), (), s32[]{:S(2)}) async-start(), calls=%async_computation.24 | async-start | bytes 5898240 | tf_op jit(solution)/shard_map/reduce_scatter | solution.py:75
  1247.1 187.7 %all-gather.26.cloned.1.call-start = ((), (), s32[]{:S(2)}) async-start(), calls=%async_computation.25 | async-start | bytes 5898240 | tf_op jit(solution)/shard_map/all_gather | solution.py:71
  1340.7 4.0 copy-start.26
  1344.7 130.0 %reduce-scatter.27.cloned.1.call-start = ((), (), s32[]{:S(2)}) async-start(), calls=%async_computation.26 | async-start | bytes 3538944 | tf_op jit(solution)/shard_map/reduce_scatter | solution.py:85
  1441.3 269.5 %all-gather.18.cloned.1.call-start = ((), (), s32[]{:S(2)}) async-start(), calls=%async_computation.18 | async-start | bytes 9437184 | tf_op jit(solution)/shard_map/all_gather | solution.py:81
  1441.4 35.6 %copy-start.6 = (bf16[1536,6,64]{0,2,1:T(8,128)(2,1)S(1)}, bf16[1536,6,64]{0,2,1:T(8,128)(2,1)}, u32[]{:S(2)}) copy-start(bf16[1536,6,64]{0,2,1:T(8,128)(2,1)} %get-tuple-element.598) | copy-start | bytes 3538948
  1441.9 339.3 %all-gather.28.cloned.1.call-start = ((), (), s32[]{:S(2)}) async-start(), calls=%async_computation.27 | async-start | bytes 10616832 | tf_op jit(solution)/shard_map/all_gather | solution.py:99
  1481.9 10.8 copy-start.11
  1507.9 20.6 copy-start.1
  1532.8 7.8 copy-start.2
  1549.7 9.2 copy-start.11
  1574.0 20.6 copy-start.1
  1599.8 7.8 copy-start.2
  1617.5 9.2 copy-start.11
  1641.8 20.6 copy-start.1
  1667.6 7.8 copy-start.2
  1685.5 2.9 copy-start.7
  1690.9 198.1 %all-reduce.8.cloned.1.call-start = ((), (), s32[]{:S(2)}) async-start(), calls=%async_computation.30 | async-start | bytes 10616832 | tf_op jit(solution)/shard_map/psum | solution.py:271
  1710.8 9.6 copy-start.41
  1725.6 8.9 copy-start.30
  1725.6 9.1 copy-start.23
  1725.6 17.1 copy-start.12
  1725.7 17.1 copy-start.37
  1725.7 251.1 %reduce-scatter.29.cloned.1.call-start = ((), (), s32[]{:S(2)}) async-start(), calls=%async_computation.28 | async-start | bytes 5898240 | tf_op jit(solution)/shard_map/reduce_scatter | solution.py:75
  1747.9 42.3 %copy-start.20 = (bf16[768,6]{0,1:T(8,128)(2,1)S(1)}, bf16[768,6]{0,1:T(8,128)(2,1)}, u32[]{:S(2)}) copy-start(bf16[768,6]{0,1:T(8,128)(2,1)} %param.21) | copy-start | bytes 27652
  1793.8 273.3 %reduce-scatter.21.cloned.1.call-start = ((), (), s32[]{:S(2)}) async-start(), calls=%async_computation.19 | async-start | bytes 5898240 | tf_op jit(solution)/shard_map/reduce_scatter | solution.py:75
  1802.9 317.9 %all-gather.30.cloned.1.call-start = ((), (), s32[]{:S(2)}) async-start(), calls=%async_computation.29 | async-start | bytes 8847360 | tf_op jit(solution)/shard_map/all_gather | solution.py:268
  1889.0 2.3 copy-start.10
  1891.3 2.1 copy-start.9
  1897.4 79.4 %copy-start.5 = (bf16[768,768]{1,0:T(8,128)(2,1)S(1)}, bf16[768,768]{1,0:T(8,128)(2,1)}, u32[]{:S(2)}) copy-start(bf16[768,768]{1,0:T(8,128)(2,1)} %param.18) | copy-start | bytes 3538948
  1897.4 79.4 %copy-start.16 = (f32[768]{0:T(1024)S(1)}, f32[768]{0:T(1024)}, u32[]{:S(2)}) copy-start(f32[768]{0:T(1024)} %copy-done.15) | copy-start | bytes 9220
  1897.4 79.4 %copy-start.21 = (f32[768]{0:T(1024)S(1)}, f32[768]{0:T(1024)}, u32[]{:S(2)}) copy-start(f32[768]{0:T(1024)} %param.19) | copy-start | bytes 9220
  1900.9 78.3 %copy-start.34 = (f32[768]{0:T(1024)S(1)}, f32[768]{0:T(1024)}, u32[]{:S(2)}) copy-start(f32[768]{0:T(1024)} %get-tuple-element.217) | copy-start | bytes 9220
  1900.9 166.1 %copy-start.14 = (f32[768]{0:T(1024)S(1)}, f32[768]{0:T(1024)}, u32[]{:S(2)}) copy-start(f32[768]{0:T(1024)} %copy-done.13) | copy-start | bytes 9220
  1900.9 166.1 %copy-start.18 = (f32[768]{0:T(1024)S(1)}, f32[768]{0:T(1024)}, u32[]{:S(2)}) copy-start(f32[768]{0:T(1024)} %param.24) | copy-start | bytes 9220
  1901.0 166.1 %copy-start.25 = (f32[768]{0:T(1024)S(1)}, f32[768]{0:T(1024)}, u32[]{:S(2)}) copy-start(f32[768]{0:T(1024)} %copy-done.24) | copy-start | bytes 9220
  1901.0 166.1 %copy-start.27 = (f32[768]{0:T(1024)S(1)}, f32[768]{0:T(1024)}, u32[]{:S(2)}) copy-start(f32[768]{0:T(1024)} %copy-done.26) | copy-start | bytes 9220
  1901.0 166.1 %copy-start.33 = (f32[768]{0:T(1024)S(1)}, f32[768]{0:T(1024)}, u32[]{:S(2)}) copy-start(f32[768]{0:T(1024)} %get-tuple-element.296) | copy-start | bytes 9220
  (8 other events, 7.5 us)
Sparse Core Ops, SparseCore 0:
  18.7 91.2 all-gather.11
  114.4 8.4 reduce-scatter.12
  125.6 161.1 reduce-scatter.10
  382.6 36.0 all-gather.13
  425.3 85.2 reduce-scatter.14
  512.0 89.9 all-gather.19
  604.1 87.8 all-gather.15
  694.3 75.5 reduce-scatter.22
  772.3 144.4 reduce-scatter.18
  919.0 144.4 reduce-scatter.16
  1073.6 80.3 all-gather.21
  1156.1 80.3 all-gather.23
  1247.2 85.2 reduce-scatter.24
  1344.8 89.9 all-gather.25
  1441.5 33.1 reduce-scatter.26
  1476.6 80.3 all-gather.17
  1691.0 90.1 all-gather.27
  1784.8 104.1 all-reduce.7
  1891.4 85.3 reduce-scatter.28
  1979.1 87.9 reduce-scatter.20
  2069.3 51.3 all-gather.29
